TPU v7x, 256 devices: a whole 4x4x8 slice. The times are simulated.
256 devices in a mesh: section: 8 (over z), dp: 32 (over y, x, core).
Axes of the slice: x: 4, y: 4, z: 8, core: 2. Of those that a mesh axis runs over, the one named last changes fastest.
Arguments:
- held: bfloat16 [8, 2, 4096, 2048], P('section', None, 'dp'), may hold values from -70 to 70
- norm_gain: float32 [8, 2048], P('section'), may hold values from 0.3 to 3
- w_qkv: bfloat16 [8, 2048, 2560], P('section', None, 'dp'), may hold values from -1 to 1
- q_gain: float32 [8, 128], P('section'), may hold values from 0.5 to 7
- k_gain: float32 [8, 128], P('section'), may hold values from 0.5 to 7
- w_out: bfloat16 [8, 2048, 2048], P('section', None, 'dp'), may hold values from -0.125 to 0.125
- lengths: int32 [8, 2, 8], P('section'), may hold values from 1 to 2048, 4096 in all within a row
Outputs:
- handed: bfloat16 [8, 2, 4096, 2048], P('section', None, 'dp')
Inputs may be any that keep to these rules, and one draw needn't show every extreme that they name: Each row lists the 8 document lengths of one packed micro-batch in order; they sum to 4096 and the longest is exactly 2048.
All inputs are finite; a program needn't handle non-finite values.
Results may differ from a plain program's by a relative error of at most 0.0086.
Values may be sent and summed in bfloat16 or wider, within the bound.
A program may use at most 128 MiB of HBM per device.

v0:
```python
import math

import jax
import jax.numpy as jnp
from jax import lax
from jax.experimental import pallas as pl
from jax.experimental.pallas import tpu as pltpu
from jax.sharding import PartitionSpec as P

HEADS = 16
KV_HEADS = 2
HEAD = 128
GROUP = 8
MICRO = 2
ROWS = 128
WIDTH = 2048
SLOTS = 32
WINDOW = 17
EPSILON = 1e-06
THETA = 1000000.0
NEGATIVE = -1e30
MESH = pl.DeviceIdType.MESH


class Gather:
    def __init__(self, piece, send_sems, recv_sems, sib_send, sib_recv, own_src=None, order=("A","B")):
        self.piece = piece
        self.ss, self.rs, self.bs, self.br = send_sems, recv_sems, sib_send, sib_recv
        me = lax.axis_index("dp")
        self.me = me
        self.c = lax.rem(me, 2)
        chip = me // 2
        self.x = lax.rem(chip, 4)
        self.y = chip // 4
        self.order = order
        self.sends = []
        self.sib_n = 0
        self.sibs = []

    def dev(self, ox, oy):
        return (lax.rem(self.y + 4 + oy, 4) * 4 + lax.rem(self.x + 4 + ox, 4)) * 2 + self.c

    def off(self, tree, first, second):
        return (first, second) if tree == "A" else (second, first)

    def role(self, tree, kind, d, k=0):
        base = 0 if tree == "A" else 20
        di = 0 if d > 0 else 1
        return base + {"1": 0, "1q": 2, "2": 4, "2q": 12}[kind] + di + 2 * k

    def copy(self, slot, tree, quarter, role, target):
        ref = self.piece(slot, tree, quarter)
        cp = pltpu.make_async_remote_copy(ref, ref, self.ss.at[role], self.rs.at[role],
            device_id={"dp": target}, device_id_type=pl.DeviceIdType.MESH)
        return cp

    def send(self, slot, tree, quarter, kind, d, k, target):
        cp = self.copy(slot, tree, quarter, self.role(tree, kind, d, k), target)
        cp.start()
        self.sends.append(cp)

    def wait(self, slot, tree, quarter, kind, d, k=0):
        self.copy(slot, tree, quarter, self.role(tree, kind, d, k), self.me).wait_recv()

    def sib_copy(self, slot, tree, n):
        ref = self.piece(slot, tree, None)
        return pltpu.make_async_remote_copy(ref, ref, self.bs.at[n], self.br.at[n],
            device_id={"dp": self.me + 1 - 2 * self.c}, device_id_type=pl.DeviceIdType.MESH)

    def to_sibling(self, slot, other, tree):
        n = self.sib_n
        self.sib_n += 1
        cp = self.sib_copy(slot, tree, n)
        cp.start()
        self.sibs.append((cp, self.sib_copy(other, tree, n)))

    FIRST = (0, -1, 1, 2)

    def slot(self, tree, first, second):
        return self.dev(*self.off(tree, first, second))

    def fan(self, tree, k, part=None):
        s = self.slot(tree, self.FIRST[k], 0)
        for d in (1, -1):
            self.send(s, tree, None, "2", d, k, self.slot(tree, 0, d))
        self.sib(s, tree)

    def sib(self, s, tree):
        if self.bs is not None:
            self.to_sibling(s, s + 1 - 2 * self.c, tree)

    def steps(self):
        out = []
        def s0():
            for t in self.order:
                for d in (1, -1):
                    self.send(self.me, t, None, "1", d, 0, self.slot(t, d, 0))
            for t in self.order:
                self.fan(t, 0)
        out.append(s0)
        def s1():
            for d in (1, -1):
                for t in self.order:
                    s = self.slot(t, -d, 0)
                    self.wait(s, t, None, "1", d)
                    self.send(s, t, 0 if d > 0 else 1, "1q", d, 0, self.slot(t, d, 0))
            for t in self.order:
                for k in (1, 2):
                    self.fan(t, k)
        out.append(s1)
        def s2():
            for t in self.order:
                s = self.slot(t, 2, 0)
                self.wait(s, t, 0, "1q", 1)
                self.wait(s, t, 1, "1q", -1)
                self.fan(t, 3)
        out.append(s2)
        def s3(k):
            def f():
                for d in (1, -1):
                    for t in self.order:
                        s = self.slot(t, self.FIRST[k], -d)
                        self.wait(s, t, None, "2", d, k)
                        self.send(s, t, 0 if d > 0 else 1, "2q", d, k, self.slot(t, 0, d))
                        self.sib(s, t)
            return f
        def s4(k):
            def f():
                for t in self.order:
                    s = self.slot(t, self.FIRST[k], 2)
                    self.wait(s, t, 0, "2q", 1, k)
                    self.wait(s, t, 1, "2q", -1, k)
                    self.sib(s, t)
            return f
        out.insert(2, s3(0))
        out += [s3(1), s4(0), s3(2), s4(1), s3(3), s4(2), s4(3)]
        return out

    def wait_siblings(self):
        for _, r in self.sibs:
            r.wait_recv()

    def finish(self):
        for cp in self.sends:
            cp.wait_send()
        for cp, _ in self.sibs:
            cp.wait_send()


def place_of(me):
    chip = me // 2
    return lax.rem(chip, 4), chip // 4, lax.rem(me, 2)


def index_of(x, y, core):
    return (lax.rem(y + 4, 4) * 4 + lax.rem(x + 4, 4)) * 2 + core


def entry_barrier(me, after, before):
    x, y, core = place_of(me)
    barrier = pltpu.get_barrier_semaphore()
    near = [
        {"dp": index_of(x + 1, y, core)},
        {"dp": index_of(x - 1, y, core)},
        {"dp": index_of(x, y + 1, core)},
        {"dp": index_of(x, y - 1, core)},
        {"dp": me + 1 - 2 * core},
        {"section": after},
        {"section": before},
    ]
    for device in near:
        pl.semaphore_signal(barrier, inc=1, device_id=device, device_id_type=MESH)
    pl.semaphore_wait(barrier, len(near))


def contract_last(left, right):
    return lax.dot_general(
        left, right, (((1,), (1,)), ((), ())), preferred_element_type=jnp.float32
    )


def relay_kernel(
    lengths,
    held_hbm,
    norm_gain,
    w_in_hbm,
    q_gain,
    k_gain,
    w_out_hbm,
    out,
    held,
    normed,
    w_in,
    w_out,
    kv_sent,
    kv,
    q_sent,
    q,
    start_sent,
    start,
    cosine,
    sine,
    residual,
    keys,
    values,
    attended,
    local_sems,
    hop_send,
    hop_recv,
    in_send,
    in_recv,
    in_out_pair,
    in_in_pair,
    kv_send,
    kv_recv,
    kv_out_pair,
    kv_in_pair,
    out_send,
    out_recv,
    out_out_pair,
    out_in_pair,
):
    me = lax.axis_index("dp")
    section = lax.axis_index("section")
    after = lax.rem(section + 1, 8)
    before = lax.rem(section + 7, 8)
    columns_in = w_in.shape[0] // SLOTS
    columns_out = w_out.shape[0] // SLOTS

    def own_rows(ref, count):
        return ref.at[pl.ds(pl.multiple_of(me * count, 16), count), :]

    held_copy = pltpu.make_async_copy(held_hbm, held, local_sems.at[0])
    held_copy.start()
    own_copy = pltpu.make_async_copy(w_in_hbm, own_rows(w_in, columns_in), local_sems.at[1])
    own_copy.start()
    entry_barrier(me, after, before)

    def hop(source, target, number):
        return pltpu.make_async_remote_copy(
            source,
            target,
            hop_send.at[number],
            hop_recv.at[number],
            device_id={"section": after},
            device_id_type=MESH,
        )

    hop_w_out = hop(w_out_hbm, own_rows(w_out, columns_out), 0)
    hop_held = hop(held_hbm, residual, 1)
    hop_start = hop(start_sent, start, 2)
    hop_kv = hop(kv_sent, kv.at[me], 3)
    hop_q = [hop(q_sent.at[h], q.at[h], 4 + h) for h in range(KV_HEADS)]
    hop_w_out.start()
    hop_held.start()

    def by_columns(ref, count):
        def piece(slot, tree, quarter):
            rows = pl.ds(pl.multiple_of(slot * count, 16), count)
            base = 0 if tree == "A" else WIDTH // 2
            if quarter is None:
                return ref.at[rows, pl.ds(base, WIDTH // 2)]
            return ref.at[rows, pl.ds(base + WIDTH // 4 * quarter, WIDTH // 4)]

        return piece

    def by_rows(slot, tree, quarter):
        base = 0 if tree == "A" else ROWS
        if quarter is None:
            return kv.at[slot, pl.ds(base, ROWS), :]
        return kv.at[slot, pl.ds(base + ROWS // 2 * quarter, ROWS // 2), :]

    gather_in = Gather(by_columns(w_in, columns_in), in_send, in_recv, in_out_pair, in_in_pair)
    gather_kv = Gather(by_rows, kv_send, kv_recv, kv_out_pair, kv_in_pair)
    gather_out = Gather(
        by_columns(w_out, columns_out), out_send, out_recv, out_out_pair, out_in_pair
    )
    steps_in, steps_kv, steps_out = gather_in.steps(), gather_kv.steps(), gather_out.steps()

    own_copy.wait()
    steps_in[0]()

    lane = lax.broadcasted_iota(jnp.int32, (ROWS, HEAD), 1)
    token = me * ROWS + lax.broadcasted_iota(jnp.int32, (ROWS, HEAD), 0)
    low = lane < HEAD // 2
    pair = jnp.where(low, lane, lane - HEAD // 2).astype(jnp.float32)
    spacing = jnp.exp(pair * (-2.0 * math.log(THETA) / HEAD))
    for m in range(MICRO):
        end = lengths[m, 0]
        first = jnp.where(end <= token, end, 0)
        for j in range(1, 8):
            end = end + lengths[m, j]
            first = jnp.where(end <= token, end, first)
        rows = pl.ds(m * ROWS, ROWS)
        start_sent[rows, :] = first
        angle = (token - first).astype(jnp.float32) * spacing
        cosine[rows, :] = jnp.cos(angle)
        turn = jnp.sin(angle)
        sine[rows, :] = jnp.where(low, -turn, turn)
    hop_start.start()

    held_copy.wait()

    def norm_rows(i, carry):
        rows = pl.ds(pl.multiple_of(i * 32, 32), 32)
        x = held[rows, :].astype(jnp.float32)
        scale = lax.rsqrt(jnp.mean(x * x, axis=-1, keepdims=True) + EPSILON)
        normed[rows, :] = (x * scale * norm_gain[...]).astype(jnp.bfloat16)
        return carry

    for number in range(1, len(steps_in)):
        if number < 5:
            lax.fori_loop(2 * (number - 1), 2 * number, norm_rows, 0)
        steps_in[number]()

    def fill_ones(i, carry):
        rows = pl.ds(pl.multiple_of(i * ROWS, ROWS), ROWS)
        values[rows, pl.ds(HEAD, HEAD)] = jnp.ones((ROWS, HEAD), jnp.bfloat16)
        return carry

    lax.fori_loop(0, WINDOW, fill_ones, 0)
    hop_w_out.wait_recv()
    steps_out[0]()
    gather_in.wait_siblings()

    def turned(u, gain):
        scale = lax.rsqrt(jnp.mean(u * u, axis=-1, keepdims=True) + EPSILON)
        u = u * scale * gain
        return (u * cosine[...] + pltpu.roll(u, HEAD // 2, 1) * sine[...]).astype(jnp.bfloat16)

    def project(first):
        rows = pl.ds(pl.multiple_of(first, 2 * HEAD), 2 * HEAD)
        return contract_last(normed[...], w_in[rows, :])

    def as_slot(h, part):
        return pl.ds((h + 2 * part) * HEAD, HEAD)

    inner = HEADS * HEAD
    found = project(inner)
    for h in range(KV_HEADS):
        kv_sent[:, as_slot(h, 0)] = turned(found[:, h * HEAD : (h + 1) * HEAD], k_gain[...])
    found = project(inner + KV_HEADS * HEAD)
    for h in range(KV_HEADS):
        kv_sent[:, as_slot(h, 1)] = found[:, h * HEAD : (h + 1) * HEAD].astype(jnp.bfloat16)
    hop_kv.start()

    def query_pair(i, h):
        found = project((h * 4 + i) * 2 * HEAD)
        for k in range(2):
            u = turned(found[:, k * HEAD : (k + 1) * HEAD], q_gain[...])
            rows = pl.ds(pl.multiple_of((2 * i + k) * ROWS, ROWS), ROWS)
            for m in range(MICRO):
                q_sent[h, m, rows, :] = u[m * ROWS : (m + 1) * ROWS]
        return h

    lax.fori_loop(0, 2, lambda i, c: (query_pair(i, 0), c)[1], 0)
    hop_kv.wait_recv()
    steps_kv[0]()
    lax.fori_loop(2, 4, lambda i, c: (query_pair(i, 0), c)[1], 0)
    hop_q[0].start()
    steps_kv[1]()
    lax.fori_loop(0, 2, lambda i, c: (query_pair(i, 1), c)[1], 0)
    steps_kv[2]()
    lax.fori_loop(2, 4, lambda i, c: (query_pair(i, 1), c)[1], 0)
    hop_q[1].start()
    for step in steps_kv[3:]:
        step()
    gather_kv.wait_siblings()
    hop_start.wait_recv()

    scaled = math.log2(math.e) / math.sqrt(HEAD)
    own_row = lax.broadcasted_iota(jnp.int32, (ROWS, HEAD), 0)
    past = jnp.where(lane <= own_row, lane, -(1 << 20))

    def window(h, m):
        def one(j, carry):
            slot = lax.rem(me + SLOTS - (WINDOW - 1) + j, SLOTS)
            rows = pl.ds(pl.multiple_of(j * ROWS, ROWS), ROWS)
            here = pl.ds(m * ROWS, ROWS)
            keys[rows, :] = kv[slot, here, as_slot(h, 0)]
            values[rows, pl.ds(0, HEAD)] = kv[slot, here, as_slot(h, 1)]
            return carry

        lax.fori_loop(0, WINDOW, one, 0)

    def attend(h, m, i):
        rows = pl.ds(pl.multiple_of(i * 2 * ROWS, 2 * ROWS), 2 * ROWS)
        score = contract_last(q[h, m, rows, :], keys[...])
        since = start[pl.ds(m * ROWS, ROWS), :] - (me - (WINDOW - 1)) * ROWS
        for k in range(2):
            blocks = []
            for j in range(WINDOW):
                u = past if j == WINDOW - 1 else lane
                part = score[k * ROWS : (k + 1) * ROWS, j * HEAD : (j + 1) * HEAD]
                blocks.append(jnp.where(u + j * HEAD >= since, part, NEGATIVE))
            top = blocks[0]
            for part in blocks[1:]:
                top = jnp.maximum(top, part)
            top = jnp.max(top, axis=-1, keepdims=True) * scaled
            weight = jnp.concatenate(
                [jnp.exp2(part * scaled - top).astype(jnp.bfloat16) for part in blocks], axis=1
            )
            summed = jnp.dot(weight, values[...], preferred_element_type=jnp.float32)
            ratio = summed[:, :HEAD] / summed[:, HEAD:]
            columns = pl.ds(pl.multiple_of((h * GROUP + 2 * i + k) * HEAD, HEAD), HEAD)
            attended[pl.ds(m * ROWS, ROWS), columns] = ratio.astype(jnp.bfloat16)

    waiting = list(steps_out[1:])
    for h in range(KV_HEADS):
        hop_q[h].wait_recv()
        for m in range(MICRO):
            window(h, m)
            for half in range(2):
                lax.fori_loop(
                    2 * half, 2 * half + 2, lambda i, c: (attend(h, m, i), c)[1], 0
                )
                for _ in range(2):
                    if waiting:
                        waiting.pop(0)()
    for step in waiting:
        step()
    gather_out.wait_siblings()
    hop_held.wait_recv()

    def output(i, carry):
        columns = pl.ds(pl.multiple_of(i * 256, 256), 256)
        mixed = contract_last(attended[...], w_out[columns, :])
        out[:, columns] = (residual[:, columns].astype(jnp.float32) + mixed).astype(jnp.bfloat16)
        return carry

    lax.fori_loop(0, WIDTH // 256, output, 0)

    for gather in (gather_in, gather_kv, gather_out):
        gather.finish()
    for one in (hop_w_out, hop_held, hop_start, hop_kv, *hop_q):
        one.wait_send()


def on_device(held, norm_gain, w_qkv, q_gain, k_gain, w_out, lengths):
    micro, rows, width = held.shape[1:]
    bf16, f32, i32 = jnp.bfloat16, jnp.float32, jnp.int32
    tokens = micro * rows
    key_width = KV_HEADS * HEAD
    hbm = pl.BlockSpec(memory_space=pl.ANY)
    vmem = pl.BlockSpec(memory_space=pltpu.VMEM)
    sems = []
    for _ in range(3):
        sems += [pltpu.SemaphoreType.DMA((n,)) for n in (40, 40, 32, 32)]
    result = pl.pallas_call(
        relay_kernel,
        out_shape=jax.ShapeDtypeStruct((tokens, width), bf16),
        in_specs=[
            pl.BlockSpec(memory_space=pltpu.SMEM), hbm, vmem, hbm, vmem, vmem, hbm,
        ],
        out_specs=vmem,
        scratch_shapes=[
            pltpu.VMEM((tokens, width), bf16),
            pltpu.VMEM((tokens, width), bf16),
            pltpu.VMEM((w_qkv.shape[2] * SLOTS, width), bf16),
            pltpu.VMEM((w_out.shape[2] * SLOTS, width), bf16),
            pltpu.VMEM((tokens, 2 * key_width), bf16),
            pltpu.VMEM((SLOTS, tokens, 2 * key_width), bf16),
            pltpu.VMEM((KV_HEADS, micro, GROUP * rows, HEAD), bf16),
            pltpu.VMEM((KV_HEADS, micro, GROUP * rows, HEAD), bf16),
            pltpu.VMEM((tokens, HEAD), i32),
            pltpu.VMEM((tokens, HEAD), i32),
            pltpu.VMEM((tokens, HEAD), f32),
            pltpu.VMEM((tokens, HEAD), f32),
            pltpu.VMEM((tokens, width), bf16),
            pltpu.VMEM((WINDOW * rows, HEAD), bf16),
            pltpu.VMEM((WINDOW * rows, 2 * HEAD), bf16),
            pltpu.VMEM((tokens, width), bf16),
            pltpu.SemaphoreType.DMA((2,)),
            pltpu.SemaphoreType.DMA((6,)),
            pltpu.SemaphoreType.DMA((6,)),
            *sems,
        ],
        compiler_params=pltpu.CompilerParams(
            collective_id=0, has_side_effects=True, vmem_limit_bytes=56 << 20
        ),
        name="relay",
    )(
        lengths[0],
        held[0].reshape(tokens, width),
        norm_gain,
        w_qkv[0].T,
        q_gain,
        k_gain,
        w_out[0].T,
    )
    return result.reshape(1, micro, rows, width)


def solution(mesh):
    in_specs = (
        P("section", None, "dp", None),
        P("section", None),
        P("section", None, "dp"),
        P("section", None),
        P("section", None),
        P("section", None, "dp"),
        P("section", None, None),
    )
    out_specs = P("section", None, "dp", None)
    return jax.shard_map(
        on_device, mesh=mesh, in_specs=in_specs, out_specs=out_specs, check_vma=False
    )
```

profile of v0, /device:TPU:1, one launch (start us, length us, event | category | flops | bytes accessed | tf_op | source)
XLA Modules:
  0.0 115.3 jit_solution(5598253415546614641)
XLA Ops:
  0.0 113.0 %relay.1 = bf16[256,2048]{1,0:T(8,128)(2,1)} custom-call(s32[2,8]{1,0:T(2,128)} %bitcast.13, bf16[256,2048]{1,0:T(8,128)(2,1)} %bitcast.10, f32[1,2048]{1,0:T(1,128)} %norm_gain.1, bf16[80,2048]{1,0:T(8,128)(2,1)} %bitcast.11, f32[1,128]{1,0:T(1,128)} %q_gain.1, f32[1,128]{1,0:T(1,128)} %k_gain.1, bf16[64,2048]{1,0:T(8,128)(2,1)} %bitcast.12), custom_call_target="tpu_custom_call" | custom-call | tf_op jit(solution)/shard_map/relay/pallas_call | solution.py:449
  113.0 2.3 %copy.9 = bf16[1,2,128,2048]{3,2,1,0:T(8,128)(2,1)} copy(bf16[1,2,128,2048]{3,2,1,0:T(8,128)(2,1)} %bitcast.9) | data formatting | bytes 2097152
where the time goes:
time: 115 us
  Pallas kernels  113 us (98%)
  local copies, waits for them, and re-layouts  2.3 us (2%)
    pallas_call x1, Pallas kernels, on_device(): pl.pallas_call(relay_kernel, out_shape=jax.ShapeDtypeStruct((tokens, widt...  113 us
    unnamed x1, local copies, waits for them, and re-layouts  2.3 us

commit v1 on v0

--- a/solution.py
+++ b/solution.py
@@ -363,8 +363,16 @@
     steps_kv[2]()
     lax.fori_loop(2, 4, lambda i, c: (query_pair(i, 1), c)[1], 0)
     hop_q[1].start()
-    for step in steps_kv[3:]:
-        step()
+    steps_kv[3]()
+    steps_kv[4]()
+    steps_kv[5]()
+    steps_kv[6]()
+    steps_kv[7]()
+    steps_kv[8]()
+    steps_out[1]()
+    steps_kv[9]()
+    steps_out[2]()
+    steps_kv[10]()
     gather_kv.wait_siblings()
     hop_start.wait_recv()
 
@@ -405,7 +413,7 @@
             columns = pl.ds(pl.multiple_of((h * GROUP + 2 * i + k) * HEAD, HEAD), HEAD)
             attended[pl.ds(m * ROWS, ROWS), columns] = ratio.astype(jnp.bfloat16)
 
-    waiting = list(steps_out[1:])
+    between = [[3], [4], [5], [6], [7], [8], [9], [10]]
     for h in range(KV_HEADS):
         hop_q[h].wait_recv()
         for m in range(MICRO):
@@ -414,11 +422,10 @@
                 lax.fori_loop(
                     2 * half, 2 * half + 2, lambda i, c: (attend(h, m, i), c)[1], 0
                 )
-                for _ in range(2):
-                    if waiting:
-                        waiting.pop(0)()
-    for step in waiting:
-        step()
+                for number in between[h * 4 + m * 2 + half]:
+                    steps_out[number]()
+    for number in []:
+        steps_out[number]()
     gather_out.wait_siblings()
     hop_held.wait_recv()
 

time: 115 us -> 108 us (0.939)
  Pallas kernels: 113 us -> 105 us
    pallas_call x1, Pallas kernels: 113 us -> 105 us  [on_device(): pl.pallas_call(relay_kernel, out_shape=jax.ShapeDtypeStruct((tokens, widt...]
where the time goes in v1:
time: 108 us
  Pallas kernels  105 us (97%)
  local copies, waits for them, and re-layouts  2.3 us (2%)
    pallas_call x1, Pallas kernels, on_device(): pl.pallas_call(relay_kernel, out_shape=jax.ShapeDtypeStruct((tokens, widt...  105 us
    unnamed x1, local copies, waits for them, and re-layouts  2.3 us

profile of v1, /device:TPU:1, one launch (start us, length us, event | category | flops | bytes accessed | tf_op | source)
XLA Modules:
  0.0 107.6 jit_solution(14230912728413891831)
XLA Ops:
  0.0 105.3 %relay.1 = bf16[256,2048]{1,0:T(8,128)(2,1)} custom-call(s32[2,8]{1,0:T(2,128)} %bitcast.13, bf16[256,2048]{1,0:T(8,128)(2,1)} %bitcast.10, f32[1,2048]{1,0:T(1,128)} %norm_gain.1, bf16[80,2048]{1,0:T(8,128)(2,1)} %bitcast.11, f32[1,128]{1,0:T(1,128)} %q_gain.1, f32[1,128]{1,0:T(1,128)} %k_gain.1, bf16[64,2048]{1,0:T(8,128)(2,1)} %bitcast.12), custom_call_target="tpu_custom_call" | custom-call | tf_op jit(solution)/shard_map/relay/pallas_call | solution.py:456
  105.3 2.3 %copy.9 = bf16[1,2,128,2048]{3,2,1,0:T(8,128)(2,1)} copy(bf16[1,2,128,2048]{3,2,1,0:T(8,128)(2,1)} %bitcast.9) | data formatting | bytes 2097152
